TPU v7x, 32 devices: a whole 2x2x4 slice. The times are simulated.
32 devices in a mesh: tm: 2 (over core), tile: 16 (over z, y, x).
Axes of the slice: x: 2, y: 2, z: 4, core: 2. Of those that a mesh axis runs over, the one named last changes fastest.
Arguments:
- features: bfloat16 [1, 8, 64, 64, 192], P(None, 'tm', 'tile'), may hold values from -60 to 60
- gain_one: float32 [192], replicated, may hold values from 0.5 to 1.5
- shift_one: float32 [192], replicated, may hold values from -3 to 3
- kernel_one: bfloat16 [3, 3, 3, 192, 192], replicated, may hold values from -0.078125 to 0.078125
- bias_one: float32 [192], replicated, may hold values from -3 to 3
- gain_two: float32 [192], replicated, may hold values from 0.5 to 1.5
- shift_two: float32 [192], replicated, may hold values from -3 to 3
- kernel_two: bfloat16 [3, 3, 3, 192, 192], replicated, may hold values from -0.078125 to 0.078125
- bias_two: float32 [192], replicated, may hold values from -3 to 3
- up_kernel: bfloat16 [3, 3, 192, 96], replicated, may hold values from -0.15625 to 0.15625
- up_bias: float32 [96], replicated, may hold values from -3 to 3
Outputs:
- decoded: bfloat16 [1, 8, 128, 64, 192], P(None, 'tm', 'tile')
All inputs are finite; a program needn't handle non-finite values.
Results may differ from a plain program's by a relative error of at most 0.009.
Values may be sent and summed in bfloat16 or wider, within the bound.
A program may use at most 128 MiB of HBM per device.

v0:
```python
import functools

import jax
import jax.numpy as jnp
from jax import lax
from jax.experimental import pallas as pl
from jax.experimental.pallas import tpu as pltpu
from jax.sharding import PartitionSpec as P

MESH = pl.DeviceIdType.MESH
G = 32
EPS = 1e-06
KP = 640
ORDER = (2, 3, 0, 1)


def split_dot(value, picks):
    m = value.shape[0]
    high = value.astype(jnp.bfloat16).astype(jnp.float32)
    rest = value - high
    mid = rest.astype(jnp.bfloat16).astype(jnp.float32)
    low = rest - mid
    terms = jnp.concatenate([high, mid, low], axis=0).astype(jnp.bfloat16)
    made = jnp.dot(terms, picks, preferred_element_type=jnp.float32)
    return made[0:m] + made[m:2 * m] + made[2 * m:3 * m]


def kernel(
    n,
    feat, g1_h, s1_h, k1, b1_h, g2_h, s2_h, k2, b2_h, uk, ub_h,
    out,
    x_ext, h_ext, j_ext, act, jact, w1, w2, wup, ukv, vecs, ubv, norm, gmap, smap, st_own, st_prev,
    loc_sem, bulk_send, bulk_recv, own_send, own_recv, prev_send, prev_recv,
):
    frames, rows, cols, chans = feat.shape
    bf16, f32 = jnp.bfloat16, jnp.float32
    tm = lax.axis_index("tm")
    tile = lax.axis_index("tile")
    up_ok = tile > 0
    down_ok = tile < n - 1
    first = tm == 0
    later = tm > 0
    above = lax.rem(tile + n - 1, n)
    below = lax.rem(tile + 1, n)
    per = chans // G
    half = chans // 2
    inverse = 1.0 / float(n * rows * cols * per)
    old = frames - 2

    def local(i, s, d):
        copy = pltpu.make_async_copy(s, d, loc_sem.at[i])
        copy.start()
        return copy

    load_x = local(0, feat, x_ext.at[pl.ds(2, frames), pl.ds(1, rows)])

    barrier = pltpu.get_barrier_semaphore()
    for d in range(n):
        to = lax.rem(tile + d, n)
        pl.semaphore_signal(barrier, inc=1, device_id=(1 - tm, to), device_id_type=MESH)
        if d:
            pl.semaphore_signal(barrier, inc=1, device_id=(tm, to), device_id_type=MESH)

    load_u = local(1, uk, ukv)
    load_v = [
        local(4 + i, ref, vecs.at[i])
        for i, ref in enumerate((g1_h, s1_h, b1_h, g2_h, s2_h, b2_h))
    ]
    load_b = local(10, ub_h, ubv)
    load_1 = local(2, k1, w1.at[:, pl.ds(0, 3 * chans)])
    load_2 = local(3, k2, w2.at[:, pl.ds(0, 3 * chans)])

    def remote(slot, i, s, d, who):
        return pltpu.make_async_remote_copy(
            src_ref=s, dst_ref=d,
            send_sem=bulk_send.at[slot, i], recv_sem=bulk_recv.at[slot, i],
            device_id=who, device_id_type=MESH,
        )

    pending = []

    def start_all(copies):
        for copy, sends, _ in copies:
            pl.when(sends)(copy.start)
        pending.extend(copies)

    def wait_all(copies):
        for copy, _, gets in copies:
            pl.when(gets)(copy.wait_recv)

    def same_rows(slot, src, row0, f0, count, dst, g0):
        f, g = pl.ds(f0, count), pl.ds(g0, count)
        return [
            (remote(slot, 0, src.at[f, row0 + rows - 1], dst.at[g, 0], (tm, below)), down_ok, up_ok),
            (remote(slot, 1, src.at[f, row0], dst.at[g, rows + 1], (tm, above)), up_ok, down_ok),
        ]

    def next_frames(slot, src, row0, f0, count, dst, g0):
        f, g = pl.ds(f0, count), pl.ds(g0, count)
        return [
            (remote(slot, 2, src.at[f, pl.ds(row0, rows)], dst.at[g, pl.ds(1, rows)], (1, tile)), first, later),
            (remote(slot, 3, src.at[f, row0 + rows - 1], dst.at[g, 0], (1, below)), first & down_ok, later & up_ok),
            (remote(slot, 4, src.at[f, row0], dst.at[g, rows + 1], (1, above)), first & up_ok, later & down_ok),
        ]

    sent = []

    def own_copy(slot, d):
        return pltpu.make_async_remote_copy(
            src_ref=st_own.at[slot, 0, pl.ds(0, 2)], dst_ref=st_own.at[slot, d, pl.ds(0, 2)],
            send_sem=own_send.at[slot], recv_sem=own_recv.at[slot],
            device_id=(tm, lax.rem(tile + d, n)), device_id_type=MESH)

    def prev_copy(slot, to_slot, d):
        return pltpu.make_async_remote_copy(
            src_ref=st_own.at[slot, 0, pl.ds(0, 2)], dst_ref=st_prev.at[to_slot, d, pl.ds(0, 2)],
            send_sem=prev_send.at[to_slot], recv_sem=prev_recv.at[to_slot],
            device_id=(1, lax.rem(tile + d, n)), device_id_type=MESH)

    def own_all(slot):
        view = st_own.at[slot, pl.ds(1, n - 1), pl.ds(0, 2)]
        return pltpu.make_async_remote_copy(
            src_ref=view, dst_ref=view, send_sem=own_send.at[slot], recv_sem=own_recv.at[slot],
            device_id=(tm, below), device_id_type=MESH)

    def prev_all(slot):
        view = st_prev.at[slot, pl.ds(0, n), pl.ds(0, 2)]
        return pltpu.make_async_remote_copy(
            src_ref=view, dst_ref=view, send_sem=prev_send.at[slot], recv_sem=prev_recv.at[slot],
            device_id=(1, below), device_id_type=MESH)

    def send_sums(slot, message, to_slot):
        st_own[slot, 0, 0:2] = message
        for d in range(1, n):
            own_copy(slot, d).start()
        if to_slot is not None:
            @pl.when(first)
            def _():
                for d in range(n):
                    prev_copy(slot, to_slot, d).start()
        sent.append((slot, to_slot))

    def sums_of(flat):
        return jnp.concatenate(
            [jnp.sum(flat, axis=0, keepdims=True), jnp.sum(flat * flat, axis=0, keepdims=True)], axis=0
        )

    def norm_from(slot, total, f, gain):
        both = split_dot(total, smap[f]) * inverse
        mean = both[0:1]
        var = both[1:2] - mean * mean
        norm[slot, 0:1] = mean
        norm[slot, 1:2] = lax.rsqrt(var + EPS) * gain

    def own_total(slot):
        return jnp.sum(st_own[slot], axis=0)[0:2]

    def prev_total(slot):
        return jnp.sum(st_prev[slot], axis=0)[0:2]

    col = lax.broadcasted_iota(jnp.int32, (cols, chans), 0)

    def put_shifted(dst, f, r, value):
        left = jnp.where(col == 0, 0.0, pltpu.roll(value, 1, 0))
        right = jnp.where(col == cols - 1, 0.0, pltpu.roll(value, cols - 1, 0))
        dst[f, r, :, 0:chans] = left.astype(bf16)
        dst[f, r, :, chans:2 * chans] = value.astype(bf16)
        dst[f, r, :, 2 * chans:3 * chans] = right.astype(bf16)

    def act_frame(src, f, shift):
        mean, scale = norm[f, 0:1], norm[f, 1:2]
        for r in range(rows + 2):
            part = 0.5 * ((src[f, r].astype(f32) - mean) * scale + shift)
            value = part + part * jnp.tanh(part)
            ok = up_ok if r == 0 else down_ok if r == rows + 1 else None
            if f < 2:
                ok = later if ok is None else ok & later
            if ok is not None:
                value = jnp.where(ok, value, 0.0)
            put_shifted(act, f, r, value)

    def conv(f, w):
        parts = [
            act[f + i, j:j + rows].reshape(rows * cols, KP) for i in range(3) for j in range(3)
        ]
        return jnp.dot(
            jnp.concatenate(parts, axis=-1), w[...].reshape(9 * KP, chans), preferred_element_type=f32
        )

    lane = lax.broadcasted_iota(jnp.int32, (chans, 128), 1)
    chan = lax.broadcasted_iota(jnp.int32, (chans, 128), 0)
    lane_t = lax.broadcasted_iota(jnp.int32, (128, chans), 0)
    chan_t = lax.broadcasted_iota(jnp.int32, (128, chans), 1)
    for f in range(frames):
        low = (lane - f * G) * per
        gmap[f] = jnp.where((chan >= low) & (chan < low + per), 1.0, 0.0).astype(bf16)
        low = (lane_t - f * G) * per
        smap[f] = jnp.where((chan_t >= low) & (chan_t < low + per), 1.0, 0.0).astype(bf16)

    load_x.wait()
    message = jnp.zeros((2, 128), f32)
    for f in range(frames):
        flat = x_ext[2 + f, 1:1 + rows].reshape(rows * cols, chans).astype(f32)
        message = message + split_dot(sums_of(flat), gmap[f])

    own_one = same_rows(0, feat, 0, 0, frames, x_ext, 2)
    prev_one = next_frames(0, feat, 0, old, 2, x_ext, 0)
    pl.semaphore_wait(barrier, 2 * n - 1)
    send_sums(0, message, 0)
    start_all(own_one + prev_one)

    pad = KP - 3 * chans
    act[:, :, :, 3 * chans:KP] = jnp.zeros((frames + 2, rows + 2, cols, pad), bf16)
    jact[:, :, :, 3 * chans:KP] = jnp.zeros((frames, rows + 2, cols, pad), bf16)
    w1[:, 3 * chans:KP] = jnp.zeros((9, pad, chans), bf16)
    w2[:, 3 * chans:KP] = jnp.zeros((9, pad, chans), bf16)
    wup[:, :, 3 * chans:KP] = jnp.zeros((2, 2, pad, chans), bf16)
    load_u.wait()
    for r in range(2):
        for dy in range(2):
            js = (((0,), (1, 2)) if r == 0 else ((0, 1), (2,)))[dy]
            line = [
                functools.reduce(jnp.add, [ukv[j, k].astype(f32) for j in js]) for k in range(3)
            ]
            zero = jnp.zeros_like(line[0])
            pieces = [(line[0], zero), (line[1] + line[2], line[0] + line[1]), (zero, line[2])]
            for dx, (even, odd) in enumerate(pieces):
                wup[r, dy, dx * chans:(dx + 1) * chans, 0:half] = even.astype(bf16)
                wup[r, dy, dx * chans:(dx + 1) * chans, half:chans] = odd.astype(bf16)
    for copy in load_v:
        copy.wait()
    load_b.wait()
    vecs[6, :, 0:half] = ubv[...]
    vecs[6, :, half:chans] = ubv[...]
    load_1.wait()

    own_all(0).wait_recv()
    wait_all(own_one)
    gain, shift = vecs[0], vecs[1]
    total = own_total(0)
    for f in range(frames):
        norm_from(2 + f, total, f, gain)

    halos = {}

    def hidden_frame(f):
        hidden = (conv(f, w1) + vecs[2]).astype(bf16)
        h_ext[2 + f, 1:1 + rows] = hidden.reshape(rows, cols, chans)
        return split_dot(sums_of(hidden.astype(f32)), gmap[0])

    def hidden_send(f, message):
        send_sums(1 + f, message, 1 + f - old if f >= old else None)
        halos[f] = same_rows(1 + f, h_ext, 1, 2 + f, 1, h_ext, 2 + f)
        ahead = []
        if f >= old:
            ahead = next_frames(1 + f, h_ext, 1, 2 + f, 1, h_ext, f - old)
            halos[f - frames] = ahead
        start_all(ahead + halos[f])

    for f in (2, 3, 4):
        act_frame(x_ext, f, shift)
    message = hidden_frame(2)
    act_frame(x_ext, 5, shift)
    hidden_send(2, message)

    @pl.when(later)
    def _():
        prev_all(0).wait_recv()

    wait_all(prev_one)
    total = prev_total(0)
    for f in range(2):
        norm_from(f, total, old + f, gain)
    message = hidden_frame(3)
    for f in range(2):
        act_frame(x_ext, f, shift)
    hidden_send(3, message)
    hidden_send(0, hidden_frame(0))
    hidden_send(1, hidden_frame(1))

    gain, shift = vecs[3], vecs[4]

    def second_frame(f):
        own_all(1 + f).wait_recv()
        wait_all(halos[f])
        norm_from(2 + f, own_total(1 + f), 0, gain)
        act_frame(h_ext, 2 + f, shift)

    def joined_frame(f):
        base = x_ext[2 + f, 1:1 + rows].reshape(rows * cols, chans).astype(f32)
        joined = (base + (conv(f, w2) + vecs[5])).astype(bf16)
        j_ext[f, 1:1 + rows] = joined.reshape(rows, cols, chans)
        copies = same_rows(1 + frames + f, j_ext, 1, f, 1, j_ext, f)
        start_all(copies)
        wide = joined.astype(f32).reshape(rows, cols, chans)
        for r in range(rows):
            put_shifted(jact, f, 1 + r, wide[r])
        return copies

    second_frame(2)
    second_frame(3)

    @pl.when(later)
    def _():
        prev_all(1).wait_recv()
        prev_all(2).wait_recv()

    for f in range(2):
        wait_all(halos[old + f - frames])
    for f in range(2):
        norm_from(f, prev_total(1 + f), 0, gain)
        act_frame(h_ext, f, shift)
    second_frame(0)
    load_2.wait()
    rims = [joined_frame(0)]
    second_frame(1)
    rims += [joined_frame(f) for f in range(1, frames)]

    bias = vecs[6]
    for f in range(frames):
        wait_all(rims[f])
        top = jnp.where(up_ok, j_ext[f, 0].astype(f32), 0.0)
        bottom = jnp.where(down_ok, j_ext[f, rows + 1].astype(f32), 0.0)
        put_shifted(jact, f, 0, top)
        put_shifted(jact, f, rows + 1, bottom)
        for r in range(2):
            parts = [jact[f, r + dy:r + dy + rows].reshape(rows * cols, KP) for dy in range(2)]
            made = jnp.dot(
                jnp.concatenate(parts, axis=-1), wup[r].reshape(2 * KP, chans), preferred_element_type=f32
            ) + bias
            made = made.astype(bf16).reshape(rows, cols, chans)
            for y in range(rows):
                out[f, 2 * y + r] = made[y]

    for copy, sends, _ in pending:
        pl.when(sends)(copy.wait_send)
    for slot, to_slot in sent:
        own_all(slot).wait_send()
    @pl.when(first)
    def _():
        for slot, to_slot in sent:
            if to_slot is not None:
                prev_all(to_slot).wait_send()


def solution(mesh):
    n = mesh.shape["tile"]

    def body(features, g1, s1, k1, b1, g2, s2, k2, b2, uk, ub):
        _, frames, rows, cols, chans = features.shape
        bf16, f32 = jnp.bfloat16, jnp.float32
        hbm = pl.BlockSpec(memory_space=pltpu.HBM)
        vec = lambda v: v.reshape(1, -1)
        dma = pltpu.SemaphoreType.DMA
        made = pl.pallas_call(
            functools.partial(kernel, n),
            out_shape=jax.ShapeDtypeStruct((frames, 2 * rows, cols, chans), bf16),
            in_specs=[hbm] * 11,
            out_specs=pl.BlockSpec(memory_space=pltpu.VMEM),
            scratch_shapes=[
                pltpu.VMEM((frames + 2, rows + 2, cols, chans), bf16),
                pltpu.VMEM((frames + 2, rows + 2, cols, chans), bf16),
                pltpu.VMEM((frames, rows + 2, cols, chans), bf16),
                pltpu.VMEM((frames + 2, rows + 2, cols, KP), bf16),
                pltpu.VMEM((frames, rows + 2, cols, KP), bf16),
                pltpu.VMEM((9, KP, chans), bf16),
                pltpu.VMEM((9, KP, chans), bf16),
                pltpu.VMEM((2, 2, KP, chans), bf16),
                pltpu.VMEM(uk.shape, bf16),
                pltpu.VMEM((7, 1, chans), f32),
                pltpu.VMEM((1, chans // 2), f32),
                pltpu.VMEM((frames + 2, 8, chans), f32),
                pltpu.VMEM((frames, chans, 128), bf16),
                pltpu.VMEM((frames, 128, chans), bf16),
                pltpu.VMEM((1 + frames, n, 8, 128), f32),
                pltpu.VMEM((3, n, 8, 128), f32),
                dma((11,)),
                dma((1 + 2 * frames, 5)),
                dma((1 + 2 * frames, 5)),
                dma((1 + frames,)),
                dma((1 + frames,)),
                dma((3,)),
                dma((3,)),
            ],
            compiler_params=pltpu.CompilerParams(
                collective_id=0, has_side_effects=True, vmem_limit_bytes=56 * 1024 * 1024
            ),
        )(
            features[0], vec(g1), vec(s1), k1.reshape(9, 3 * chans, chans), vec(b1),
            vec(g2), vec(s2), k2.reshape(9, 3 * chans, chans), vec(b2), uk, vec(ub),
        )
        return made[None]

    return jax.shard_map(
        body,
        mesh=mesh,
        in_specs=(P(None, "tm", "tile", None, None),) + (P(),) * 10,
        out_specs=P(None, "tm", "tile", None, None),
        check_vma=False,
    )
```

profile of v0, /device:TPU:0, one launch (start us, length us, event | category | flops | bytes accessed | tf_op | source)
XLA Modules:
  0.0 42.5 jit_solution(2792973630715110824)
XLA Ops:
  0.0 40.2 %shard_map.109 = bf16[4,8,64,192]{3,2,1,0:T(8,128)(2,1)} custom-call(bf16[4,4,64,192]{3,2,1,0:T(8,128)(2,1)} %bitcast.14, f32[1,192]{1,0:T(1,128)} %bitcast.15, f32[1,192]{1,0:T(1,128)} %bitcast.16, bf16[9,576,192]{2,1,0:T(8,128)(2,1)} %bitcast.12, f32[1,192]{1,0:T(1,128)} %bitcast.17, f32[1,192]{1,0:T(1,128)} %bitcast.18, f32[1,192]{1,0:T(1,128)} %bitcast.19, ...), custom_call_target="tpu_custom_call" | custom-call | tf_op jit(solution)/shard_map/pallas_call | solution.py:355
  40.2 2.3 %copy.13 = bf16[1,4,8,64,192]{4,3,2,1,0:T(8,128)(2,1)} copy(bf16[1,4,8,64,192]{4,3,2,1,0:T(8,128)(2,1)} %bitcast.11) | data formatting | bytes 1572864
where the time goes:
time: 42.7 us; the launch traced here: 42.5 us
  Pallas kernels  40.2 us (94%)
  local copies, waits for them, and re-layouts  2.3 us (5%)
    pallas_call x1, Pallas kernels, body(): pl.pallas_call(functools.partial(kernel, n), out_shape=jax.ShapeDtypeStru...  40.2 us
    unnamed x1, local copies, waits for them, and re-layouts  2.3 us

commit v1 on v0

--- a/solution.py
+++ b/solution.py
@@ -29,7 +29,7 @@
     n,
     feat, g1_h, s1_h, k1, b1_h, g2_h, s2_h, k2, b2_h, uk, ub_h,
     out,
-    x_ext, h_ext, j_ext, act, jact, w1, w2, wup, ukv, vecs, ubv, norm, gmap, smap, st_own, st_prev,
+    x_ext, h_ext, j_ext, act, jact, w1, w2, wup, ukv, vecs, ubv, norm, gmap, smap, st_own, st_prev, st_fwd, beside,
     loc_sem, bulk_send, bulk_recv, own_send, own_recv, prev_send, prev_recv,
 ):
     frames, rows, cols, chans = feat.shape
@@ -55,11 +55,11 @@
     load_x = local(0, feat, x_ext.at[pl.ds(2, frames), pl.ds(1, rows)])
 
     barrier = pltpu.get_barrier_semaphore()
-    for d in range(n):
+    for d in range(1, n):
         to = lax.rem(tile + d, n)
+        pl.semaphore_signal(barrier, inc=1, device_id=(tm, to), device_id_type=MESH)
+    for to in (tile, above, below):
         pl.semaphore_signal(barrier, inc=1, device_id=(1 - tm, to), device_id_type=MESH)
-        if d:
-            pl.semaphore_signal(barrier, inc=1, device_id=(tm, to), device_id_type=MESH)
 
     load_u = local(1, uk, ukv)
     load_v = [
@@ -111,11 +111,15 @@
             send_sem=own_send.at[slot], recv_sem=own_recv.at[slot],
             device_id=(tm, lax.rem(tile + d, n)), device_id_type=MESH)
 
-    def prev_copy(slot, to_slot, d):
+    def forward(slot):
         return pltpu.make_async_remote_copy(
-            src_ref=st_own.at[slot, 0, pl.ds(0, 2)], dst_ref=st_prev.at[to_slot, d, pl.ds(0, 2)],
-            send_sem=prev_send.at[to_slot], recv_sem=prev_recv.at[to_slot],
-            device_id=(1, lax.rem(tile + d, n)), device_id_type=MESH)
+            src_ref=st_fwd.at[slot, pl.ds(0, 2)], dst_ref=st_prev.at[slot, pl.ds(0, 2)],
+            send_sem=prev_send.at[slot], recv_sem=prev_recv.at[slot],
+            device_id=(1, tile), device_id_type=MESH)
+
+    def send_total(slot, total):
+        st_fwd[slot, 0:2] = total
+        pl.when(first)(forward(slot).start)
 
     def own_all(slot):
         view = st_own.at[slot, pl.ds(1, n - 1), pl.ds(0, 2)]
@@ -123,22 +127,11 @@
             src_ref=view, dst_ref=view, send_sem=own_send.at[slot], recv_sem=own_recv.at[slot],
             device_id=(tm, below), device_id_type=MESH)
 
-    def prev_all(slot):
-        view = st_prev.at[slot, pl.ds(0, n), pl.ds(0, 2)]
-        return pltpu.make_async_remote_copy(
-            src_ref=view, dst_ref=view, send_sem=prev_send.at[slot], recv_sem=prev_recv.at[slot],
-            device_id=(1, below), device_id_type=MESH)
-
-    def send_sums(slot, message, to_slot):
+    def send_sums(slot, message):
         st_own[slot, 0, 0:2] = message
         for d in range(1, n):
             own_copy(slot, d).start()
-        if to_slot is not None:
-            @pl.when(first)
-            def _():
-                for d in range(n):
-                    prev_copy(slot, to_slot, d).start()
-        sent.append((slot, to_slot))
+        sent.append(slot)
 
     def sums_of(flat):
         return jnp.concatenate(
@@ -150,19 +143,21 @@
         mean = both[0:1]
         var = both[1:2] - mean * mean
         norm[slot, 0:1] = mean
-        norm[slot, 1:2] = lax.rsqrt(var + EPS) * gain
+        norm[slot, 1:2] = 0.5 * (lax.rsqrt(var + EPS) * gain)
 
     def own_total(slot):
         return jnp.sum(st_own[slot], axis=0)[0:2]
 
     def prev_total(slot):
-        return jnp.sum(st_prev[slot], axis=0)[0:2]
-
-    col = lax.broadcasted_iota(jnp.int32, (cols, chans), 0)
+        return st_prev[slot, 0:2]
+
+    beside[:, 0:8] = jnp.zeros((rows + 2, 8, chans), f32)
+    beside[:, 8 + cols:16 + cols] = jnp.zeros((rows + 2, 8, chans), f32)
 
     def put_shifted(dst, f, r, value):
-        left = jnp.where(col == 0, 0.0, pltpu.roll(value, 1, 0))
-        right = jnp.where(col == cols - 1, 0.0, pltpu.roll(value, cols - 1, 0))
+        beside[r, 8:8 + cols] = value
+        left = beside[r, 7:7 + cols]
+        right = beside[r, 9:9 + cols]
         dst[f, r, :, 0:chans] = left.astype(bf16)
         dst[f, r, :, chans:2 * chans] = value.astype(bf16)
         dst[f, r, :, 2 * chans:3 * chans] = right.astype(bf16)
@@ -170,7 +165,7 @@
     def act_frame(src, f, shift):
         mean, scale = norm[f, 0:1], norm[f, 1:2]
         for r in range(rows + 2):
-            part = 0.5 * ((src[f, r].astype(f32) - mean) * scale + shift)
+            part = (src[f, r].astype(f32) - mean) * scale + shift
             value = part + part * jnp.tanh(part)
             ok = up_ok if r == 0 else down_ok if r == rows + 1 else None
             if f < 2:
@@ -205,8 +200,8 @@
 
     own_one = same_rows(0, feat, 0, 0, frames, x_ext, 2)
     prev_one = next_frames(0, feat, 0, old, 2, x_ext, 0)
-    pl.semaphore_wait(barrier, 2 * n - 1)
-    send_sums(0, message, 0)
+    pl.semaphore_wait(barrier, n + 2)
+    send_sums(0, message)
     start_all(own_one + prev_one)
 
     pad = KP - 3 * chans
@@ -236,8 +231,9 @@
 
     own_all(0).wait_recv()
     wait_all(own_one)
-    gain, shift = vecs[0], vecs[1]
+    gain, shift = vecs[0], 0.5 * vecs[1]
     total = own_total(0)
+    send_total(0, total)
     for f in range(frames):
         norm_from(2 + f, total, f, gain)
 
@@ -249,7 +245,7 @@
         return split_dot(sums_of(hidden.astype(f32)), gmap[0])
 
     def hidden_send(f, message):
-        send_sums(1 + f, message, 1 + f - old if f >= old else None)
+        send_sums(1 + f, message)
         halos[f] = same_rows(1 + f, h_ext, 1, 2 + f, 1, h_ext, 2 + f)
         ahead = []
         if f >= old:
@@ -265,7 +261,7 @@
 
     @pl.when(later)
     def _():
-        prev_all(0).wait_recv()
+        forward(0).wait_recv()
 
     wait_all(prev_one)
     total = prev_total(0)
@@ -278,12 +274,14 @@
     hidden_send(0, hidden_frame(0))
     hidden_send(1, hidden_frame(1))
 
-    gain, shift = vecs[3], vecs[4]
+    gain, shift = vecs[3], 0.5 * vecs[4]
 
     def second_frame(f):
-        own_all(1 + f).wait_recv()
+        if f < old:
+            own_all(1 + f).wait_recv()
+            totals[f] = own_total(1 + f)
         wait_all(halos[f])
-        norm_from(2 + f, own_total(1 + f), 0, gain)
+        norm_from(2 + f, totals[f], 0, gain)
         act_frame(h_ext, 2 + f, shift)
 
     def joined_frame(f):
@@ -297,13 +295,18 @@
             put_shifted(jact, f, 1 + r, wide[r])
         return copies
 
+    totals = {}
+    for f in range(old, frames):
+        own_all(1 + f).wait_recv()
+        totals[f] = own_total(1 + f)
+        send_total(1 + f - old, totals[f])
     second_frame(2)
     second_frame(3)
 
     @pl.when(later)
     def _():
-        prev_all(1).wait_recv()
-        prev_all(2).wait_recv()
+        forward(1).wait_recv()
+        forward(2).wait_recv()
 
     for f in range(2):
         wait_all(halos[old + f - frames])
@@ -334,13 +337,13 @@
 
     for copy, sends, _ in pending:
         pl.when(sends)(copy.wait_send)
-    for slot, to_slot in sent:
+    for slot in sent:
         own_all(slot).wait_send()
+
     @pl.when(first)
     def _():
-        for slot, to_slot in sent:
-            if to_slot is not None:
-                prev_all(to_slot).wait_send()
+        for slot in range(3):
+            forward(slot).wait_send()
 
 
 def solution(mesh):
@@ -373,7 +376,9 @@
                 pltpu.VMEM((frames, chans, 128), bf16),
                 pltpu.VMEM((frames, 128, chans), bf16),
                 pltpu.VMEM((1 + frames, n, 8, 128), f32),
-                pltpu.VMEM((3, n, 8, 128), f32),
+                pltpu.VMEM((3, 8, 128), f32),
+                pltpu.VMEM((3, 8, 128), f32),
+                pltpu.VMEM((rows + 2, cols + 16, chans), f32),
                 dma((11,)),
                 dma((1 + 2 * frames, 5)),
                 dma((1 + 2 * frames, 5)),

time: 42.7 us -> 41.6 us (0.974)
  Pallas kernels: 40.2 us -> 39.1 us
    pallas_call x1, Pallas kernels: 40.2 us -> 39.1 us  [body(): pl.pallas_call(functools.partial(kernel, n), out_shape=jax.ShapeDtypeStru...]
where the time goes in v1:
time: 41.6 us; the launch traced here: 41.4 us
  Pallas kernels  39.1 us (94%)
  local copies, waits for them, and re-layouts  2.3 us (6%)
    pallas_call x1, Pallas kernels, body(): pl.pallas_call(functools.partial(kernel, n), out_shape=jax.ShapeDtypeStru...  39.1 us
    unnamed x1, local copies, waits for them, and re-layouts  2.3 us

profile of v1, /device:TPU:0, one launch (start us, length us, event | category | flops | bytes accessed | tf_op | source)
XLA Modules:
  0.0 41.4 jit_solution(12137243645352596291)
XLA Ops:
  0.0 39.1 %shard_map.109 = bf16[4,8,64,192]{3,2,1,0:T(8,128)(2,1)} custom-call(bf16[4,4,64,192]{3,2,1,0:T(8,128)(2,1)} %bitcast.14, f32[1,192]{1,0:T(1,128)} %bitcast.15, f32[1,192]{1,0:T(1,128)} %bitcast.16, bf16[9,576,192]{2,1,0:T(8,128)(2,1)} %bitcast.12, f32[1,192]{1,0:T(1,128)} %bitcast.17, f32[1,192]{1,0:T(1,128)} %bitcast.18, f32[1,192]{1,0:T(1,128)} %bitcast.19, ...), custom_call_target="tpu_custom_call" | custom-call | tf_op jit(solution)/shard_map/pallas_call | solution.py:358
  39.1 2.3 %copy.13 = bf16[1,4,8,64,192]{4,3,2,1,0:T(8,128)(2,1)} copy(bf16[1,4,8,64,192]{4,3,2,1,0:T(8,128)(2,1)} %bitcast.11) | data formatting | bytes 1572864

commit v2 on v1

--- a/solution.py
+++ b/solution.py
@@ -272,7 +272,6 @@
         act_frame(x_ext, f, shift)
     hidden_send(3, message)
     hidden_send(0, hidden_frame(0))
-    hidden_send(1, hidden_frame(1))
 
     gain, shift = vecs[3], 0.5 * vecs[4]
 
@@ -296,12 +295,16 @@
         return copies
 
     totals = {}
-    for f in range(old, frames):
+
+    def pass_on(f):
         own_all(1 + f).wait_recv()
         totals[f] = own_total(1 + f)
         send_total(1 + f - old, totals[f])
+
+    pass_on(2)
     second_frame(2)
-    second_frame(3)
+    hidden_send(1, hidden_frame(1))
+    pass_on(3)
 
     @pl.when(later)
     def _():
@@ -315,6 +318,7 @@
         act_frame(h_ext, f, shift)
     second_frame(0)
     load_2.wait()
+    second_frame(3)
     rims = [joined_frame(0)]
     second_frame(1)
     rims += [joined_frame(f) for f in range(1, frames)]

time: 41.6 us -> 42.1 us (1.012)
  Pallas kernels: 39.1 us -> 39.7 us
    pallas_call x1, Pallas kernels: 39.1 us -> 39.7 us  [body(): pl.pallas_call(functools.partial(kernel, n), out_shape=jax.ShapeDtypeStru...]
where the time goes in v2:
time: 42.1 us; the launch traced here: 42 us
  Pallas kernels  39.7 us (94%)
  local copies, waits for them, and re-layouts  2.3 us (5%)
    pallas_call x1, Pallas kernels, body(): pl.pallas_call(functools.partial(kernel, n), out_shape=jax.ShapeDtypeStru...  39.7 us
    unnamed x1, local copies, waits for them, and re-layouts  2.3 us

profile of v2, /device:TPU:0, one launch (start us, length us, event | category | flops | bytes accessed | tf_op | source)
XLA Modules:
  0.0 42.0 jit_solution(126544132678989038)
XLA Ops:
  0.0 39.7 %shard_map.109 = bf16[4,8,64,192]{3,2,1,0:T(8,128)(2,1)} custom-call(bf16[4,4,64,192]{3,2,1,0:T(8,128)(2,1)} %bitcast.14, f32[1,192]{1,0:T(1,128)} %bitcast.15, f32[1,192]{1,0:T(1,128)} %bitcast.16, bf16[9,576,192]{2,1,0:T(8,128)(2,1)} %bitcast.12, f32[1,192]{1,0:T(1,128)} %bitcast.17, f32[1,192]{1,0:T(1,128)} %bitcast.18, f32[1,192]{1,0:T(1,128)} %bitcast.19, ...), custom_call_target="tpu_custom_call" | custom-call | tf_op jit(solution)/shard_map/pallas_call | solution.py:362
  39.7 2.3 %copy.13 = bf16[1,4,8,64,192]{4,3,2,1,0:T(8,128)(2,1)} copy(bf16[1,4,8,64,192]{4,3,2,1,0:T(8,128)(2,1)} %bitcast.11) | data formatting | bytes 1572864
